TPU v7x, 32 devices: a whole 2x2x4 slice. The times are simulated.
32 devices in a mesh: segment: 4 (over y, x), seq: 8 (over z, core).
Axes of the slice: x: 2, y: 2, z: 4, core: 2. Of those that a mesh axis runs over, the one named last changes fastest.
Arguments:
- hidden: bfloat16 [4, 8192, 8192], P('segment', 'seq'), may hold values from -6 to 6
- span_lengths: int32 [4, 64], replicated, may hold values from 1 to 512, 8192 in all within a row
- section_of: int32 [4, 64], replicated, may hold values from 0 to 31
- section_live: int32 [32], P('seq'), may hold values 0 or 1
- w_in: bfloat16 [8192, 2048], P('seq'), may hold values from -0.5 to 0.5
- norm_gain: float32 [2048], replicated, may hold values from 0.5 to 1.5
- w_query: bfloat16 [2048, 2048], P(None, 'segment'), may hold values from -0.125 to 0.125
- w_key: bfloat16 [2048, 2048], P(None, 'segment'), may hold values from -0.125 to 0.125
- w_value: bfloat16 [2048, 2048], P(None, 'segment'), may hold values from -0.125 to 0.125
- w_out: bfloat16 [2048, 2048], P('segment'), may hold values from -0.125 to 0.125
Outputs:
- section_out: bfloat16 [32, 2048], P('seq')
All inputs are finite; a program needn't handle non-finite values. No bound on the sum of `section_live` on one device may be relied on, other than what follows from the above.
Results may differ from a plain program's by a relative error of at most 0.007.
Values may be sent and summed in bfloat16 or wider, within the bound.
A program may use at most 128 MiB of HBM per device.

v0:
```python
import jax
import jax.numpy as jnp
from jax import lax
from jax.sharding import PartitionSpec as P

HEAD_DIM = 128


def shards(
    hidden, span_lengths, section_of, section_live, w_in, norm_gain, w_query, w_key, w_value, w_out
):
    tokens = hidden[0]
    seq_count = lax.axis_size("seq")
    seq_index = lax.axis_index("seq")
    segment_index = lax.axis_index("segment")
    tok_count = tokens.shape[0]
    lengths = lax.dynamic_index_in_dim(span_lengths, segment_index, 0, keepdims=False)
    span_ends = jnp.cumsum(lengths)
    span_starts = span_ends - lengths
    positions = seq_index * tok_count + jnp.arange(tok_count, dtype=jnp.int32)
    member = (
        (positions[None, :] >= span_starts[:, None]) & (positions[None, :] < span_ends[:, None])
    ).astype(jnp.bfloat16)
    partial_value = jnp.dot(member, tokens, preferred_element_type=jnp.float32)
    length_float = lengths.astype(jnp.float32)
    sections_here = section_live.shape[0]
    section_total = sections_here * seq_count
    section_ids = jnp.arange(section_total, dtype=jnp.int32)
    own_sections = seq_index * sections_here + jnp.arange(sections_here, dtype=jnp.int32)
    flat_sections = section_of.reshape(-1)
    count_all = jnp.sum(
        (section_ids[:, None] == flat_sections[None, :]).astype(jnp.float32), axis=1
    )
    doc_sections = lax.dynamic_index_in_dim(section_of, segment_index, 0, keepdims=False)
    weighted = partial_value / length_float[:, None]
    doc_onehot = (section_ids[:, None] == doc_sections[None, :]).astype(jnp.float32)
    section_part = jnp.dot(doc_onehot, weighted, precision=lax.Precision.HIGHEST)
    feature_block = lax.psum_scatter(section_part, "seq", scatter_dimension=1, tiled=True)
    doc_total = lax.psum(feature_block, "segment")
    pooled = (doc_total / jnp.maximum(count_all, 1.0)[:, None]).astype(jnp.bfloat16)
    projected = jnp.dot(pooled, w_in, preferred_element_type=jnp.float32)
    section_in = lax.psum_scatter(projected, "seq", scatter_dimension=0, tiled=True)
    scale = lax.rsqrt(jnp.mean(section_in * section_in, axis=1, keepdims=True) + 1e-05)
    normed = (section_in * scale * norm_gain[None, :]).astype(jnp.bfloat16)
    queries = jnp.dot(normed, w_query, preferred_element_type=jnp.float32).astype(jnp.bfloat16)
    keys_here = jnp.dot(normed, w_key, preferred_element_type=jnp.float32).astype(jnp.bfloat16)
    values_here = jnp.dot(normed, w_value, preferred_element_type=jnp.float32).astype(jnp.bfloat16)
    live_here = section_live.astype(jnp.bfloat16)
    keys_all, values_all, live_all = (
        lax.all_gather(keys_here, "seq", axis=0, tiled=True),
        lax.all_gather(values_here, "seq", axis=0, tiled=True),
        lax.all_gather(live_here, "seq", axis=0, tiled=True),
    )
    local_heads = queries.shape[1] // HEAD_DIM
    query_heads = queries.reshape(sections_here, local_heads, HEAD_DIM)
    key_heads = keys_all.reshape(section_total, local_heads, HEAD_DIM)
    value_heads = values_all.reshape(section_total, local_heads, HEAD_DIM)
    scores = jnp.einsum("qhd,khd->hqk", query_heads, key_heads, preferred_element_type=jnp.float32)
    scores = scores / jnp.sqrt(jnp.float32(HEAD_DIM))
    allowed = (live_all[None, :] > 0) | (section_ids[None, :] == own_sections[:, None])
    scores = jnp.where(allowed[None, :, :], scores, jnp.float32(-1e30))
    probs = jax.nn.softmax(scores, axis=-1).astype(jnp.bfloat16)
    attended = jnp.einsum(
        "hqk,khd->qhd", probs, value_heads, preferred_element_type=jnp.float32
    ).astype(jnp.bfloat16)
    attended = attended.reshape(sections_here, local_heads * HEAD_DIM)
    head_terms = jnp.dot(attended, w_out, preferred_element_type=jnp.float32)
    combined = lax.psum(head_terms, "segment")
    return (section_in + combined).astype(jnp.bfloat16)


def solution(mesh):
    in_specs = (
        P("segment", "seq", None),
        P(),
        P(),
        P("seq"),
        P("seq", None),
        P(),
        P(None, "segment"),
        P(None, "segment"),
        P(None, "segment"),
        P("segment", None),
    )
    out_specs = P("seq", None)
    return jax.shard_map(shards, mesh=mesh, in_specs=in_specs, out_specs=out_specs, check_vma=False)
```

profile of v0, /device:TPU:0, one launch (start us, length us, event | category | flops | bytes accessed | tf_op | source)
XLA Modules:
  0.0 217.7 jit_solution(10877947771555918930)
XLA Ops:
  6.5 0.0 copy-start
  6.5 0.0 reduce-scatter.2.cloned.1.call-start
  6.5 0.9 fusion.30
  7.4 0.1 copy.25
  7.5 0.1 reduce-window.7
  7.6 0.1 reduce
  7.7 0.7 bitcast_subtract_fusion
  8.4 8.8 %fusion.3 = f32[64,8192]{1,0:T(8,128)S(1)} fusion(bf16[1,1024,8192]{2,1,0:T(8,128)(2,1)} %param.10, f32[64]{0:T(128)S(1)} %get-tuple-element.6, s32[1024]{0:T(1024)S(1)} %iota_add_fusion, s32[64]{0:T(128)S(1)} %reduce, s32[64]{0:T(128)S(1)} %bitcast_subtract_fusion), kind=kOutput, calls=%fused_computation.3 | convolution fusion | flops 1074462720 | bytes 18879232 | tf_op jit(solution)/shard_map/dot_general | solution.py:24
  17.3 0.0 copy-start.2
  17.3 0.0 copy-start.4
  17.3 0.0 copy-start.3
  17.3 1.8 fusion.25
  19.1 0.0 reduce-scatter.2.cloned.1.call-update
  19.1 0.0 all-reduce.5.cloned.1.call-start
  19.2 0.0 copy-done.2
  19.2 0.1 eq.52
  19.3 0.0 copy-done.4
  19.3 0.0 copy-done.3
  19.3 0.7 fusion.31
  20.6 0.2 dynamic-update-slice
  20.9 18.2 %all-reduce = bf16[32]{0:T(256)(128)(2,1)S(1)} all-reduce(bf16[32]{0:T(256)(128)(2,1)S(1)} %dynamic-update-slice), channel_id=1, replica_groups=mesh['segment'=4,'seq'=8] {'seq'}, use_global_device_ids=true, to_apply=%add | all-reduce | flops 32 | bytes 128
  39.1 0.1 convert_reduce_fusion
  39.2 15.9 %reduce-scatter.2.cloned.1.call-done = f32[32,1024]{1,0:T(8,128)} async-done(((f32[32,8192]{1,0:T(8,128)}), f32[32,1024]{1,0:T(8,128)}) %reduce-scatter.2.cloned.1.call-update) | async-done | bytes 131088 | tf_op jit(solution)/shard_map/reduce_scatter | solution.py:38
  55.1 0.0 all-reduce.5.cloned.1.call-update
  55.1 0.0 all-reduce.7.cloned.1.call-start
  55.8 0.0 copy-start.1
  55.8 42.1 %all-reduce.5.cloned.1.call-done = f32[32,1024]{1,0:T(8,128)} async-done(((f32[32,1024]{1,0:T(8,128)}), f32[32,1024]{1,0:T(8,128)}) %all-reduce.5.cloned.1.call-update) | async-done | bytes 131088 | tf_op jit(solution)/shard_map/psum | solution.py:39
  97.9 3.8 %fusion.20 = f32[32,2048]{1,0:T(8,128)} fusion(bf16[1024,2048]{1,0:T(8,128)(2,1)} %param.14, f32[32,1024]{1,0:T(8,128)} %all-reduce.5.cloned.1.call-done, f32[32]{0:T(128)S(1)} %broadcast_maximum_fusion), kind=kOutput, calls=%fused_computation.24 | convolution fusion | flops 134283264 | bytes 4587648 | tf_op jit(solution)/shard_map/dot_general | solution.py:41
  101.7 0.0 all-reduce.7.cloned.1.call-update
  101.7 0.1 fusion.29
  101.8 55.5 %all-reduce.7.cloned.1.call-done = f32[32,2048]{1,0:T(8,128)} async-done(((f32[32,2048]{1,0:T(8,128)}), f32[32,2048]{1,0:T(8,128)}) %all-reduce.7.cloned.1.call-update) | async-done | bytes 262160
  157.3 1.0 multiply_reduce_fusion
  158.3 0.0 copy-done.1
  158.3 2.0 fusion.11
  160.3 14.1 %all-gather.1 = bf16[8,4,512]{2,1,0:T(4,128)(2,1)S(1)} all-gather(bf16[1,4,512]{2,1,0:T(4,128)(2,1)S(1)} %fusion.11), channel_id=1, replica_groups=mesh['segment'=4,'seq'=8] {'seq'}, dimensions={0}, use_global_device_ids=true | all-gather | bytes 36864 | tf_op jit(solution)/shard_map/all_gather | solution.py:50
  174.4 2.2 fusion.8
  176.6 0.2 fusion.32
  176.8 2.1 fusion.9
  178.8 14.1 %all-gather = bf16[8,4,512]{2,1,0:T(4,128)(2,1)S(1)} all-gather(bf16[1,4,512]{2,1,0:T(4,128)(2,1)S(1)} %fusion.9), channel_id=1, replica_groups=mesh['segment'=4,'seq'=8] {'seq'}, dimensions={0}, use_global_device_ids=true | all-gather | bytes 36864 | tf_op jit(solution)/shard_map/all_gather | solution.py:51
  192.9 0.0 copy-done
  193.0 0.5 fusion.13
  193.5 16.2 %psum.15 = f32[4,2048]{1,0:T(4,128)S(1)} all-reduce(f32[4,2048]{1,0:T(4,128)S(1)} %fusion.13), channel_id=1, replica_groups=mesh['segment'=4,'seq'=8] {'segment'}, use_global_device_ids=true, to_apply=%region_8.9 | all-reduce | flops 8192 | bytes 65536 | tf_op jit(solution)/shard_map/psum | solution.py:68
  209.7 1.5 add_convert_fusion
  (9 shorter events, 0.1 us)
Async XLA Ops:
  6.5 186.4 %copy-start = (bf16[512,2048]{1,0:T(8,128)(2,1)S(1)}, bf16[512,2048]{1,0:T(8,128)(2,1)}, u32[]{:S(2)}) copy-start(bf16[512,2048]{1,0:T(8,128)(2,1)} %param.19) | copy-start | bytes 6291460
  6.5 48.5 %reduce-scatter.2.cloned.1.call-start = ((), (), s32[]{:S(2)}) async-start(), calls=%async_computation.1 | async-start | bytes 1179648 | tf_op jit(solution)/shard_map/reduce_scatter | solution.py:38
  17.3 1.9 copy-start.2
  17.3 2.0 copy-start.4
  17.3 2.0 copy-start.3
  19.1 78.7 %all-reduce.5.cloned.1.call-start = ((), (), s32[]{:S(2)}) async-start(), calls=%async_computation.2 | async-start | bytes 262144 | tf_op jit(solution)/shard_map/psum | solution.py:39
  55.1 102.2 %all-reduce.7.cloned.1.call-start = ((), (), s32[]{:S(2)}) async-start(), calls=%async_computation.3 | async-start | bytes 524288
  55.8 102.5 %copy-start.1 = (f32[2048]{0:T(1024)S(1)}, f32[2048]{0:T(1024)}, u32[]{:S(2)}) copy-start(f32[2048]{0:T(1024)} %param.15) | copy-start | bytes 24580
Sparse Core Ops, SparseCore 0:
  19.3 35.7 reduce-scatter.1
  58.0 39.8 all-reduce.4
  101.9 55.4 all-reduce.6
where the time goes:
time: 218 us
  waiting for transfers between devices  113 us (52%)
  blocking collectives  62.6 us (29%)
  matrix products  21.3 us (10%)
  between operations  14.5 us (7%)
  other arithmetic  4.58 us (2%)
    unnamed x4, waiting for transfers between devices  55.5 us
    psum x1, waiting for transfers between devices, shards(): doc_total = lax.psum(feature_block, 'segment')  42.1 us
    unnamed x1, blocking collectives  18.2 us
    psum x1, blocking collectives, shards(): combined = lax.psum(head_terms, 'segment')  16.2 us
    reduce_scatter x1, waiting for transfers between devices, shards(): lax.psum_scatter(section_part, 'seq', scatter_dimension=1, tiled=True)  15.9 us
    all_gather x1, blocking collectives, shards(): lax.all_gather(keys_here, 'seq', axis=0, tiled=True)  14.1 us
    all_gather x1, blocking collectives, shards(): lax.all_gather(values_here, 'seq', axis=0, tiled=True)  14.1 us
    dot_general x1, matrix products, shards(): partial_value = jnp.dot(member, tokens, preferred_element_type=jnp.float32)  8.85 us
  transfers between devices with their start and end apart: 3, of which 3 were waited for; matrix products, arithmetic and copies ran while one was open for 1% of the time, Pallas kernels for 0%

commit v1 on v0

--- a/solution.py
+++ b/solution.py
@@ -4,6 +4,27 @@
 from jax.sharding import PartitionSpec as P
 
 HEAD_DIM = 128
+
+
+def ring_gather(shard, axis, dim):
+    length, index, rows = (lax.axis_size(axis), lax.axis_index(axis), shard.shape[dim])
+    right = [(i, (i + 1) % length) for i in range(length)]
+    downward = [(i, (i - 1) % length) for i in range(length)]
+    result = jnp.zeros((*shard.shape[:dim], length * rows, *shard.shape[dim + 1 :]), shard.dtype)
+    result = lax.dynamic_update_slice_in_dim(result, shard, index * rows, axis=dim)
+    from_left = from_right = shard
+    halfway = length // 2
+    for step in range(1, halfway + 1):
+        from_left = lax.ppermute(from_left, axis, right)
+        result = lax.dynamic_update_slice_in_dim(
+            result, from_left, (index - step) % length * rows, axis=dim
+        )
+        if step < length - halfway:
+            from_right = lax.ppermute(from_right, axis, downward)
+            result = lax.dynamic_update_slice_in_dim(
+                result, from_right, (index + step) % length * rows, axis=dim
+            )
+    return result
 
 
 def shards(
@@ -47,7 +68,7 @@
     values_here = jnp.dot(normed, w_value, preferred_element_type=jnp.float32).astype(jnp.bfloat16)
     live_here = section_live.astype(jnp.bfloat16)
     keys_all, values_all, live_all = (
-        lax.all_gather(keys_here, "seq", axis=0, tiled=True),
+        ring_gather(keys_here, "seq", 0),
         lax.all_gather(values_here, "seq", axis=0, tiled=True),
         lax.all_gather(live_here, "seq", axis=0, tiled=True),
     )

time: 218 us -> 222 us (1.018)
  blocking collectives: 62.6 us -> 48.6 us
  starting transfers between devices: 0.08 us -> 10.7 us
  waiting for transfers between devices: 113 us -> 121 us
    all_gather x1 -> x0, blocking collectives: 14.1 us -> none  [shards(): lax.all_gather(keys_here, 'seq', axis=0, tiled=True)]
    ppermute x0 -> x7, starting transfers between devices: none -> 10.6 us  [the longest x3 10.2 us: ring_gather(): from_right = lax.ppermute(from_right, axis, downward)]
    ppermute x0 -> x7, waiting for transfers between devices: none -> 7.37 us  [the longest x4 7.3 us: ring_gather(): from_left = lax.ppermute(from_left, axis, right)]
  transfers between devices with their start and end apart: 3 -> 10, of which waited for: 3 -> 6; matrix products, arithmetic and copies ran while one was open for 1% -> 1% of each run, Pallas kernels for 0% -> 0%
where the time goes in v1:
time: 222 us
  waiting for transfers between devices  121 us (55%)
  blocking collectives  48.6 us (22%)
  matrix products  21.3 us (10%)
  between operations  14.7 us (7%)
  starting transfers between devices  10.7 us (5%)
  other arithmetic  4.73 us (2%)
    unnamed x4, waiting for transfers between devices  55.5 us
    psum x1, waiting for transfers between devices, shards(): doc_total = lax.psum(feature_block, 'segment')  41.9 us
    unnamed x1, blocking collectives  18.2 us
    psum x1, blocking collectives, shards(): combined = lax.psum(head_terms, 'segment')  16.3 us
    reduce_scatter x1, waiting for transfers between devices, shards(): lax.psum_scatter(section_part, 'seq', scatter_dimension=1, tiled=True)  15.9 us
    all_gather x1, blocking collectives, shards(): lax.all_gather(values_here, 'seq', axis=0, tiled=True)  14.1 us
    ppermute x3, starting transfers between devices, ring_gather(): from_right = lax.ppermute(from_right, axis, downward)  10.2 us
    dot_general x1, matrix products, shards(): partial_value = jnp.dot(member, tokens, preferred_element_type=jnp.float32)  8.85 us
  transfers between devices with their start and end apart: 10, of which 6 were waited for; matrix products, arithmetic and copies ran while one was open for 1% of the time, Pallas kernels for 0%

profile of v1, /device:TPU:0, one launch (start us, length us, event | category | flops | bytes accessed | tf_op | source)
XLA Modules:
  0.0 222.0 jit_solution(16816890030447267579)
XLA Ops:
  6.5 0.0 copy-start
  6.5 0.0 reduce-scatter.2.cloned.1.call-start
  6.5 0.9 fusion.31
  7.4 0.1 copy.25
  7.5 0.1 reduce-window.7
  7.6 0.1 reduce
  7.7 0.7 bitcast_subtract_fusion
  8.4 8.8 %fusion.3 = f32[64,8192]{1,0:T(8,128)S(1)} fusion(bf16[1,1024,8192]{2,1,0:T(8,128)(2,1)} %param.10, f32[64]{0:T(128)S(1)} %get-tuple-element.6, s32[1024]{0:T(1024)S(1)} %iota_add_fusion, s32[64]{0:T(128)S(1)} %reduce, s32[64]{0:T(128)S(1)} %bitcast_subtract_fusion), kind=kOutput, calls=%fused_computation.3 | convolution fusion | flops 1074462720 | bytes 18879232 | tf_op jit(solution)/shard_map/dot_general | solution.py:45
  17.3 0.0 copy-start.3
  17.3 0.0 copy-start.5
  17.3 0.0 copy-start.4
  17.3 1.8 fusion.25
  19.1 0.0 reduce-scatter.2.cloned.1.call-update
  19.1 0.0 all-reduce.5.cloned.1.call-start
  19.2 0.0 copy-done.3
  19.2 0.1 eq.60
  19.3 0.0 copy-done.5
  19.3 0.0 copy-done.4
  19.3 0.7 fusion.32
  20.6 0.2 dynamic-update-slice
  20.9 18.2 %all-reduce = bf16[32]{0:T(256)(128)(2,1)S(1)} all-reduce(bf16[32]{0:T(256)(128)(2,1)S(1)} %dynamic-update-slice), channel_id=1, replica_groups=mesh['segment'=4,'seq'=8] {'seq'}, use_global_device_ids=true, to_apply=%add | all-reduce | flops 32 | bytes 128
  39.1 0.1 convert_reduce_fusion
  39.2 15.9 %reduce-scatter.2.cloned.1.call-done = f32[32,1024]{1,0:T(8,128)} async-done(((f32[32,8192]{1,0:T(8,128)}), f32[32,1024]{1,0:T(8,128)}) %reduce-scatter.2.cloned.1.call-update) | async-done | bytes 131088 | tf_op jit(solution)/shard_map/reduce_scatter | solution.py:59
  55.1 0.0 all-reduce.5.cloned.1.call-update
  55.1 0.0 all-reduce.7.cloned.1.call-start
  55.9 0.0 copy-start.2
  56.0 41.9 %all-reduce.5.cloned.1.call-done = f32[32,1024]{1,0:T(8,128)} async-done(((f32[32,1024]{1,0:T(8,128)}), f32[32,1024]{1,0:T(8,128)}) %all-reduce.5.cloned.1.call-update) | async-done | bytes 131088 | tf_op jit(solution)/shard_map/psum | solution.py:60
  97.9 3.8 %fusion.19 = f32[32,2048]{1,0:T(8,128)} fusion(bf16[1024,2048]{1,0:T(8,128)(2,1)} %param.14, f32[32,1024]{1,0:T(8,128)} %all-reduce.5.cloned.1.call-done, f32[32]{0:T(128)S(1)} %broadcast_maximum_fusion), kind=kOutput, calls=%fused_computation.23 | convolution fusion | flops 134283264 | bytes 4587648 | tf_op jit(solution)/shard_map/dot_general | solution.py:62
  101.7 0.0 all-reduce.7.cloned.1.call-update
  101.7 0.1 fusion.29
  101.8 55.5 %all-reduce.7.cloned.1.call-done = f32[32,2048]{1,0:T(8,128)} async-done(((f32[32,2048]{1,0:T(8,128)}), f32[32,2048]{1,0:T(8,128)}) %all-reduce.7.cloned.1.call-update) | async-done | bytes 262160
  157.3 0.0 copy-start.1
  157.3 1.1 multiply_reduce_fusion
  158.4 0.0 copy-done
  158.5 0.0 copy-done.2
  158.5 1.3 constant_dynamic-update-slice_fusion.7
  159.7 0.0 collective-permute-start
  159.7 3.5 %collective-permute-start.1 = (bf16[4,512]{1,0:T(4,128)(2,1)S(1)}, bf16[4,512]{1,0:T(4,128)(2,1)S(1)}, u32[]{:S(2)}, u32[]{:S(2)}) collective-permute-start(bf16[4,512]{1,0:T(4,128)(2,1)S(1)} %get-tuple-element.10), channel_id=1, source_target_pairs={{0,7},{1,0},{2,1},{3,2},{4,3},{5,4},{6,5},{7,6},{8,15},{9,8},{10,9... | collective-permute-start | bytes 12296 | tf_op jit(solution)/shard_map/ppermute | solution.py:23
  163.3 0.0 copy-done.1
  163.3 1.3 fusion.9
  164.5 14.1 %all-gather = bf16[8,4,512]{2,1,0:T(4,128)(2,1)S(1)} all-gather(bf16[1,4,512]{2,1,0:T(4,128)(2,1)S(1)} %fusion.9), channel_id=1, replica_groups=mesh['segment'=4,'seq'=8] {'seq'}, dimensions={0}, use_global_device_ids=true | all-gather | bytes 36864 | tf_op jit(solution)/shard_map/all_gather | solution.py:72
  178.6 0.0 collective-permute-done
  178.7 0.4 collective-permute-start.2
  179.1 0.0 collective-permute-done.1
  179.1 3.2 %collective-permute-start.3 = (bf16[4,512]{1,0:T(4,128)(2,1)S(1)}, bf16[4,512]{1,0:T(4,128)(2,1)S(1)}, u32[]{:S(2)}, u32[]{:S(2)}) collective-permute-start(bf16[4,512]{1,0:T(4,128)(2,1)S(1)} %collective-permute-done.1), channel_id=1, source_target_pairs={{0,7},{1,0},{2,1},{3,2},{4,3},{5,4},{6,5},{7,6},{8,15},{9,8},{10,9... | collective-permute-start | bytes 12296 | tf_op jit(solution)/shard_map/ppermute | solution.py:23
  182.3 1.3 collective-permute-done.2
  183.5 0.0 collective-permute-start.4
  183.5 0.0 collective-permute-done.3
  183.6 3.5 %collective-permute-start.5 = (bf16[4,512]{1,0:T(4,128)(2,1)S(1)}, bf16[4,512]{1,0:T(4,128)(2,1)S(1)}, u32[]{:S(2)}, u32[]{:S(2)}) collective-permute-start(bf16[4,512]{1,0:T(4,128)(2,1)S(1)} %collective-permute-done.3), channel_id=1, source_target_pairs={{0,7},{1,0},{2,1},{3,2},{4,3},{5,4},{6,5},{7,6},{8,15},{9,8},{10,9... | collective-permute-start | bytes 12296 | tf_op jit(solution)/shard_map/ppermute | solution.py:23
  187.1 1.3 collective-permute-done.4
  188.4 0.0 collective-permute-start.6
  188.4 0.0 collective-permute-done.5
  188.4 4.8 %collective-permute-done.6 = bf16[4,512]{1,0:T(4,128)(2,1)S(1)} collective-permute-done((bf16[4,512]{1,0:T(4,128)(2,1)S(1)}, bf16[4,512]{1,0:T(4,128)(2,1)S(1)}, u32[]{:S(2)}, u32[]{:S(2)}) %collective-permute-start.6) | collective-permute-done | bytes 4128 | tf_op jit(solution)/shard_map/ppermute | solution.py:18
  193.2 2.2 fusion.8
  195.4 0.2 fusion.33
  195.5 2.2 fusion.12
  197.7 16.3 %psum.15 = f32[4,2048]{1,0:T(4,128)S(1)} all-reduce(f32[4,2048]{1,0:T(4,128)S(1)} %fusion.12), channel_id=1, replica_groups=mesh['segment'=4,'seq'=8] {'segment'}, use_global_device_ids=true, to_apply=%region_8.9 | all-reduce | flops 8192 | bytes 65536 | tf_op jit(solution)/shard_map/psum | solution.py:89
  214.0 1.5 add_convert_fusion
  (16 shorter events, 0.1 us)
Async XLA Ops:
  6.5 151.9 %copy-start = (bf16[2048,512]{1,0:T(8,128)(2,1)S(1)}, bf16[2048,512]{1,0:T(8,128)(2,1)}, u32[]{:S(2)}) copy-start(bf16[2048,512]{1,0:T(8,128)(2,1)} %param.17) | copy-start | bytes 6291460
  6.5 48.5 %reduce-scatter.2.cloned.1.call-start = ((), (), s32[]{:S(2)}) async-start(), calls=%async_computation.1 | async-start | bytes 1179648 | tf_op jit(solution)/shard_map/reduce_scatter | solution.py:59
  17.3 1.9 copy-start.3
  17.3 2.0 copy-start.5
  17.3 2.0 copy-start.4
  19.1 78.7 %all-reduce.5.cloned.1.call-start = ((), (), s32[]{:S(2)}) async-start(), calls=%async_computation.2 | async-start | bytes 262144 | tf_op jit(solution)/shard_map/psum | solution.py:60
  55.1 102.2 %all-reduce.7.cloned.1.call-start = ((), (), s32[]{:S(2)}) async-start(), calls=%async_computation.3 | async-start | bytes 524288
  55.9 102.5 %copy-start.2 = (f32[2048]{0:T(1024)S(1)}, f32[2048]{0:T(1024)}, u32[]{:S(2)}) copy-start(f32[2048]{0:T(1024)} %param.15) | copy-start | bytes 24580
  157.3 6.0 %copy-start.1 = (bf16[2048,512]{1,0:T(8,128)(2,1)S(1)}, bf16[2048,512]{1,0:T(8,128)(2,1)}, u32[]{:S(2)}) copy-start(bf16[2048,512]{1,0:T(8,128)(2,1)} %param.18) | copy-start | bytes 6291460
  159.7 18.9 %collective-permute-start = (bf16[4,512]{1,0:T(4,128)(2,1)S(1)}, bf16[4,512]{1,0:T(4,128)(2,1)S(1)}, u32[]{:S(2)}, u32[]{:S(2)}) collective-permute-start(bf16[4,512]{1,0:T(4,128)(2,1)S(1)} %get-tuple-element.10), channel_id=1, source_target_pairs={{0,1},{1,2},{2,3},{3,4},{4,5},{5,6},{6,7},{7,0},{8,9},{9,10},{10,1... | collective-permute-start | bytes 12296 | tf_op jit(solution)/shard_map/ppermute | solution.py:18
  159.7 19.3 %collective-permute-start.1 = (bf16[4,512]{1,0:T(4,128)(2,1)S(1)}, bf16[4,512]{1,0:T(4,128)(2,1)S(1)}, u32[]{:S(2)}, u32[]{:S(2)}) collective-permute-start(bf16[4,512]{1,0:T(4,128)(2,1)S(1)} %get-tuple-element.10), channel_id=1, source_target_pairs={{0,7},{1,0},{2,1},{3,2},{4,3},{5,4},{6,5},{7,6},{8,15},{9,8},{10,9... | collective-permute-start | bytes 12296 | tf_op jit(solution)/shard_map/ppermute | solution.py:23
  178.7 4.9 %collective-permute-start.2 = (bf16[4,512]{1,0:T(4,128)(2,1)S(1)}, bf16[4,512]{1,0:T(4,128)(2,1)S(1)}, u32[]{:S(2)}, u32[]{:S(2)}) collective-permute-start(bf16[4,512]{1,0:T(4,128)(2,1)S(1)} %collective-permute-done), channel_id=1, source_target_pairs={{0,1},{1,2},{2,3},{3,4},{4,5},{5,6},{6,7},{7,0},{8,9},{9,10},{10,1... | collective-permute-start | bytes 12296 | tf_op jit(solution)/shard_map/ppermute | solution.py:18
  179.1 4.5 %collective-permute-start.3 = (bf16[4,512]{1,0:T(4,128)(2,1)S(1)}, bf16[4,512]{1,0:T(4,128)(2,1)S(1)}, u32[]{:S(2)}, u32[]{:S(2)}) collective-permute-start(bf16[4,512]{1,0:T(4,128)(2,1)S(1)} %collective-permute-done.1), channel_id=1, source_target_pairs={{0,7},{1,0},{2,1},{3,2},{4,3},{5,4},{6,5},{7,6},{8,15},{9,8},{10,9... | collective-permute-start | bytes 12296 | tf_op jit(solution)/shard_map/ppermute | solution.py:23
  183.5 4.8 %collective-permute-start.4 = (bf16[4,512]{1,0:T(4,128)(2,1)S(1)}, bf16[4,512]{1,0:T(4,128)(2,1)S(1)}, u32[]{:S(2)}, u32[]{:S(2)}) collective-permute-start(bf16[4,512]{1,0:T(4,128)(2,1)S(1)} %collective-permute-done.2), channel_id=1, source_target_pairs={{0,1},{1,2},{2,3},{3,4},{4,5},{5,6},{6,7},{7,0},{8,9},{9,10},{10,1... | collective-permute-start | bytes 12296 | tf_op jit(solution)/shard_map/ppermute | solution.py:18
  183.6 4.8 %collective-permute-start.5 = (bf16[4,512]{1,0:T(4,128)(2,1)S(1)}, bf16[4,512]{1,0:T(4,128)(2,1)S(1)}, u32[]{:S(2)}, u32[]{:S(2)}) collective-permute-start(bf16[4,512]{1,0:T(4,128)(2,1)S(1)} %collective-permute-done.3), channel_id=1, source_target_pairs={{0,7},{1,0},{2,1},{3,2},{4,3},{5,4},{6,5},{7,6},{8,15},{9,8},{10,9... | collective-permute-start | bytes 12296 | tf_op jit(solution)/shard_map/ppermute | solution.py:23
  188.4 4.8 %collective-permute-start.6 = (bf16[4,512]{1,0:T(4,128)(2,1)S(1)}, bf16[4,512]{1,0:T(4,128)(2,1)S(1)}, u32[]{:S(2)}, u32[]{:S(2)}) collective-permute-start(bf16[4,512]{1,0:T(4,128)(2,1)S(1)} %collective-permute-done.4), channel_id=1, source_target_pairs={{0,1},{1,2},{2,3},{3,4},{4,5},{5,6},{6,7},{7,0},{8,9},{9,10},{10,1... | collective-permute-start | bytes 12296 | tf_op jit(solution)/shard_map/ppermute | solution.py:18
Sparse Core Ops, SparseCore 0:
  19.3 35.7 reduce-scatter.1
  58.0 39.8 all-reduce.4
  101.9 55.4 all-reduce.6
